TPU v7x, 128 devices: a whole 4x4x4 slice. The times are simulated.
128 devices in a mesh: dom: 32 (over y, x, core), near: 4 (over z).
Axes of the slice: x: 4, y: 4, z: 4, core: 2. Of those that a mesh axis runs over, the one named last changes fastest.
Arguments:
- start_block: float32 [131072, 128], P(('dom', 'near')), may hold values from -6 to 6
- near_tiles: float32 [6144, 128, 128], P(('dom', 'near')), may hold values from -0.09375 to 0.09375
- near_src: int32 [6144], P(('dom', 'near')), may hold values from 0 to 31, as said below
- near_mask: int32 [6144], P(('dom', 'near')), may hold values 0 or 1
- far_tiles: float32 [1024, 128, 128], P(('dom', 'near')), may hold values from -0.09375 to 0.09375
- far_src: int32 [1024], P(('dom', 'near')), may hold values from 0 to 31
- far_mask: int32 [1024], P(('dom', 'near')), may hold values 0 or 1
- bound_count: int32 [128], P(('dom', 'near')), may hold values from 1 to 128
Outputs:
- encodings: float32 [131072, 128], P(('dom', 'near'))
- rayleigh: float32 [128, 128], replicated
Inputs may be any that keep to these rules, and one draw needn't show every extreme that they name: `near_src`: each partition holds 48 consecutive slots; the slot at position j among them (j from 0) lies in tile row j // 6; the first slot of each tile row reads the partition's own tile of that row; every source tile from another partition of the group is one of that partition's first 4 tiles.
All inputs are finite; a program needn't handle non-finite values. No bound on the sum of `near_mask` or of `far_mask` on one device may be relied on, other than what follows from the above.
Results may differ from a plain program's by a relative error of at most 0.0003.
Values sent between devices are 32-bit elements; how exact they have to be, the bound alone decides.
No kernel may reach another device: no remote copies, remote signals or barrier semaphores. Data moves between devices by JAX's collectives and lax.ppermute only.
A program may use at most 64 MiB of HBM per device.

v0:
```python
from functools import partial
import jax
import jax.numpy as jnp
from jax import lax
from jax.sharding import PartitionSpec as P

NPER = 6
ITERS = 2
DEG = 3
LOWER_EDGE = 0.6
UPPER_EDGE = 2.0


def apply_operator(
    block, near_tiles, near_src, near_mask, far_tiles, far_src, far_mask, bound_count
):
    tile_rows = near_tiles.shape[1]
    width = block.shape[1]
    tiles_dev = block.shape[0] // tile_rows
    group_size = lax.axis_size("near")
    gathered = lax.all_gather(block, "near", axis=0, tiled=True)
    picked = gathered.reshape(group_size * tiles_dev, tile_rows, width)[near_src]
    products = jnp.einsum("sij,sjk->sik", near_tiles, picked, precision=lax.Precision.HIGHEST)
    products = products * near_mask.astype(jnp.float32)[:, None, None]
    near_sum = products.reshape(tiles_dev, NPER, tile_rows, width).sum(axis=1)
    limit = (jnp.arange(tile_rows) < bound_count[0]).astype(jnp.float32)
    edge_tile = block[:tile_rows] * limit[:, None]
    edges = lax.all_gather(edge_tile, "dom", axis=0, tiled=True).reshape(
        lax.axis_size("dom"), tile_rows, width
    )
    far_pick = edges[far_src]
    far_sum = jnp.einsum("sij,sjk->sik", far_tiles, far_pick, precision=lax.Precision.HIGHEST)
    far_sum = far_sum * far_mask.astype(jnp.float32)[:, None, None]
    return block - (near_sum + far_sum).reshape(block.shape)


def chebyshev(current, image, operator):
    center = (UPPER_EDGE + LOWER_EDGE) / 2.0
    half = (UPPER_EDGE - LOWER_EDGE) / 2.0
    previous = current
    present = (image - center * current) / half
    for degree in range(DEG - 1):
        following = 2.0 * (operator(present) - center * present) / half - previous
        previous, present = (present, following)
    return present


def inner(left, right):
    return jnp.dot(
        left.T, right, precision=lax.Precision.HIGHEST, preferred_element_type=jnp.float32
    )


def times_inverse(block, lower_inv):
    return jnp.dot(
        block, lower_inv.T, precision=lax.Precision.HIGHEST, preferred_element_type=jnp.float32
    )


def inverse_factor(gram):
    lower = jnp.linalg.cholesky(gram)
    return jax.scipy.linalg.solve_triangular(
        lower, jnp.eye(gram.shape[0], dtype=jnp.float32), lower=True
    )


def local(start_block, near_tiles, near_src, near_mask, far_tiles, far_src, far_mask, bound_count):
    operator = partial(
        apply_operator,
        near_tiles=near_tiles,
        near_src=near_src,
        near_mask=near_mask,
        far_tiles=far_tiles,
        far_src=far_src,
        far_mask=far_mask,
        bound_count=bound_count,
    )
    nodes_all = start_block.shape[0] * lax.axis_size("dom") * lax.axis_size("near")
    current = start_block
    image = operator(current)
    for iteration in range(ITERS):
        if iteration > 0:
            image = operator(current)
        filtered = chebyshev(current, image, operator)
        gram = lax.psum(inner(filtered, filtered), ("dom", "near")) / nodes_all
        lower_inv = inverse_factor(gram)
        current = times_inverse(filtered, lower_inv)
    final_image = operator(current)
    rayleigh = lax.psum(inner(current, final_image), ("dom", "near")) / nodes_all
    return (current, rayleigh)


def solution(mesh):
    return jax.shard_map(
        local,
        mesh=mesh,
        in_specs=(
            P(("dom", "near"), None),
            P(("dom", "near"), None, None),
            P(("dom", "near")),
            P(("dom", "near")),
            P(("dom", "near"), None, None),
            P(("dom", "near")),
            P(("dom", "near")),
            P(("dom", "near")),
        ),
        out_specs=(P(("dom", "near"), None), P()),
        check_vma=False,
    )
```

profile of v0, /device:TPU:1, one launch (start us, length us, event | category | flops | bytes accessed | tf_op | source)
XLA Modules:
  0.0 1082.7 jit_solution(1137057290617790462)
XLA Ops:
  13.1 30.7 %all-gather.15.cloned.1.call-done = f32[4096,128]{1,0:T(8,128)} async-done(((f32[1024,128]{1,0:T(8,128)}), f32[4096,128]{1,0:T(8,128)}) %all-gather.15.cloned.1.call-update) | async-done | bytes 2097168 | tf_op jit(solution)/shard_map/all_gather | solution.py:21
  47.7 8.1 convolution_multiply_fusion.6
  60.8 29.6 %all-gather.17.cloned.1.call-done = f32[4096,128]{1,0:T(8,128)} async-done(((f32[128,128]{1,0:T(8,128)}), f32[4096,128]{1,0:T(8,128)}) %all-gather.17.cloned.1.call-update) | async-done | bytes 2097168 | tf_op jit(solution)/shard_map/all_gather | solution.py:28
  99.8 28.3 %all-gather.19.cloned.1.call-done = f32[4096,128]{1,0:T(8,128)} async-done(((f32[1024,128]{1,0:T(8,128)}), f32[4096,128]{1,0:T(8,128)}) %all-gather.19.cloned.1.call-update) | async-done | bytes 2097168 | tf_op jit(solution)/shard_map/all_gather | solution.py:21
  145.2 29.5 %all-gather.21.cloned.1.call-done = f32[4096,128]{1,0:T(8,128)} async-done(((f32[128,128]{1,0:T(8,128)}), f32[4096,128]{1,0:T(8,128)}) %all-gather.21.cloned.1.call-update) | async-done | bytes 2097168 | tf_op jit(solution)/shard_map/all_gather | solution.py:28
  184.5 28.1 %all-gather.23.cloned.1.call-done = f32[4096,128]{1,0:T(8,128)} async-done(((f32[1024,128]{1,0:T(8,128)}), f32[4096,128]{1,0:T(8,128)}) %all-gather.23.cloned.1.call-update) | async-done | bytes 2097168 | tf_op jit(solution)/shard_map/all_gather | solution.py:21
  216.5 8.1 convolution_multiply_fusion.4
  229.7 29.5 %all-gather.25.cloned.1.call-done = f32[4096,128]{1,0:T(8,128)} async-done(((f32[128,128]{1,0:T(8,128)}), f32[4096,128]{1,0:T(8,128)}) %all-gather.25.cloned.1.call-update) | async-done | bytes 2097168 | tf_op jit(solution)/shard_map/all_gather | solution.py:28
  268.2 138.8 %all-reduce.4.cloned.1.call-done = f32[128,128]{0,1:T(8,128)} async-done(((f32[128,128]{0,1:T(8,128)}), f32[128,128]{0,1:T(8,128)}) %all-reduce.4.cloned.1.call-update) | async-done | bytes 65552 | tf_op jit(solution)/shard_map/psum | solution.py:85
  408.8 11.7 %cholesky.44 = f32[128,128]{1,0:T(8,128)S(1)} custom-call(f32[128,128]{1,0:T(8,128)S(1)} %fusion.41), custom_call_target="Cholesky" | custom-call | tf_op jit(solution)/shard_map/jit(cholesky)/cholesky | solution.py:61
  421.9 9.8 custom-call.6
  436.1 26.2 %all-gather.27.cloned.1.call-done = f32[4096,128]{1,0:T(8,128)} async-done(((f32[1024,128]{1,0:T(8,128)}), f32[4096,128]{1,0:T(8,128)}) %all-gather.27.cloned.1.call-update) | async-done | bytes 2097168 | tf_op jit(solution)/shard_map/all_gather | solution.py:21
  466.3 8.1 convolution_multiply_fusion.3
  479.4 29.6 %all-gather.29.cloned.1.call-done = f32[4096,128]{1,0:T(8,128)} async-done(((f32[128,128]{1,0:T(8,128)}), f32[4096,128]{1,0:T(8,128)}) %all-gather.29.cloned.1.call-update) | async-done | bytes 2097168 | tf_op jit(solution)/shard_map/all_gather | solution.py:28
  518.6 28.1 %all-gather.31.cloned.1.call-done = f32[4096,128]{1,0:T(8,128)} async-done(((f32[1024,128]{1,0:T(8,128)}), f32[4096,128]{1,0:T(8,128)}) %all-gather.31.cloned.1.call-update) | async-done | bytes 2097168 | tf_op jit(solution)/shard_map/all_gather | solution.py:21
  563.8 29.6 %all-gather.33.cloned.1.call-done = f32[4096,128]{1,0:T(8,128)} async-done(((f32[128,128]{1,0:T(8,128)}), f32[4096,128]{1,0:T(8,128)}) %all-gather.33.cloned.1.call-update) | async-done | bytes 2097168 | tf_op jit(solution)/shard_map/all_gather | solution.py:28
  603.0 28.3 %all-gather.35.cloned.1.call-done = f32[4096,128]{1,0:T(8,128)} async-done(((f32[1024,128]{1,0:T(8,128)}), f32[4096,128]{1,0:T(8,128)}) %all-gather.35.cloned.1.call-update) | async-done | bytes 2097168 | tf_op jit(solution)/shard_map/all_gather | solution.py:21
  648.4 29.6 %all-gather.37.cloned.1.call-done = f32[4096,128]{1,0:T(8,128)} async-done(((f32[128,128]{1,0:T(8,128)}), f32[4096,128]{1,0:T(8,128)}) %all-gather.37.cloned.1.call-update) | async-done | bytes 2097168 | tf_op jit(solution)/shard_map/all_gather | solution.py:28
  687.5 138.4 %all-reduce.6.cloned.1.call-done = f32[128,128]{0,1:T(8,128)} async-done(((f32[128,128]{0,1:T(8,128)}), f32[128,128]{0,1:T(8,128)}) %all-reduce.6.cloned.1.call-update) | async-done | bytes 65552 | tf_op jit(solution)/shard_map/psum | solution.py:85
  827.7 11.7 %cholesky.55 = f32[128,128]{1,0:T(8,128)S(1)} custom-call(f32[128,128]{1,0:T(8,128)S(1)} %fusion.39), custom_call_target="Cholesky" | custom-call | tf_op jit(solution)/shard_map/jit(cholesky)/cholesky | solution.py:61
  840.8 9.8 custom-call.7
  855.2 26.0 %all-gather.39.cloned.1.call-done = f32[4096,128]{1,0:T(8,128)} async-done(((f32[1024,128]{1,0:T(8,128)}), f32[4096,128]{1,0:T(8,128)}) %all-gather.39.cloned.1.call-update) | async-done | bytes 2097168 | tf_op jit(solution)/shard_map/all_gather | solution.py:21
  898.3 29.5 %all-gather.41.cloned.1.call-done = f32[4096,128]{1,0:T(8,128)} async-done(((f32[128,128]{1,0:T(8,128)}), f32[4096,128]{1,0:T(8,128)}) %all-gather.41.cloned.1.call-update) | async-done | bytes 2097168 | tf_op jit(solution)/shard_map/all_gather | solution.py:28
  935.5 138.9 %all-reduce.8.cloned.1.call-done = f32[128,128]{0,1:T(8,128)} async-done(((f32[128,128]{0,1:T(8,128)}), f32[128,128]{0,1:T(8,128)}) %all-reduce.8.cloned.1.call-update) | async-done | bytes 65552 | tf_op jit(solution)/shard_map/psum | solution.py:89
  (128 shorter events, 181.6 us)
Async XLA Ops:
  7.2 40.5 %copy-start = (f32[48,128,128]{2,1,0:T(8,128)S(1)}, f32[48,128,128]{2,1,0:T(8,128)}, u32[]{:S(2)}) copy-start(f32[48,128,128]{2,1,0:T(8,128)} %param.12) | copy-start | bytes 9437188
  7.2 36.5 %all-gather.15.cloned.1.call-start = ((), (), s32[]{:S(2)}) async-start(), calls=%async_computation | async-start | bytes 2621440 | tf_op jit(solution)/shard_map/all_gather | solution.py:21
  7.9 82.5 %all-gather.17.cloned.1.call-start = ((), (), s32[]{:S(2)}) async-start(), calls=%async_computation.1 | async-start | bytes 2162688 | tf_op jit(solution)/shard_map/all_gather | solution.py:28
  10.4 117.7 %all-gather.19.cloned.1.call-start = ((), (), s32[]{:S(2)}) async-start(), calls=%async_computation.2 | async-start | bytes 2621440 | tf_op jit(solution)/shard_map/all_gather | solution.py:21
  95.4 0.8 copy-start.2
  98.1 76.5 %all-gather.21.cloned.1.call-start = ((), (), s32[]{:S(2)}) async-start(), calls=%async_computation.3 | async-start | bytes 2162688 | tf_op jit(solution)/shard_map/all_gather | solution.py:28
  99.8 112.8 %all-gather.23.cloned.1.call-start = ((), (), s32[]{:S(2)}) async-start(), calls=%async_computation.4 | async-start | bytes 2621440 | tf_op jit(solution)/shard_map/all_gather | solution.py:21
  179.6 0.8 copy-start.6
  182.6 76.5 %all-gather.25.cloned.1.call-start = ((), (), s32[]{:S(2)}) async-start(), calls=%async_computation.5 | async-start | bytes 2162688 | tf_op jit(solution)/shard_map/all_gather | solution.py:28
  184.2 222.8 %all-reduce.4.cloned.1.call-start = ((), (), s32[]{:S(2)}) async-start(), calls=%async_computation.6 | async-start | bytes 131072 | tf_op jit(solution)/shard_map/psum | solution.py:85
  265.7 0.8 copy-start.4
  268.1 194.2 %all-gather.27.cloned.1.call-start = ((), (), s32[]{:S(2)}) async-start(), calls=%async_computation.7 | async-start | bytes 2621440 | tf_op jit(solution)/shard_map/all_gather | solution.py:21
  434.5 74.6 %all-gather.29.cloned.1.call-start = ((), (), s32[]{:S(2)}) async-start(), calls=%async_computation.8 | async-start | bytes 2162688 | tf_op jit(solution)/shard_map/all_gather | solution.py:28
  436.1 110.6 %all-gather.31.cloned.1.call-start = ((), (), s32[]{:S(2)}) async-start(), calls=%async_computation.9 | async-start | bytes 2621440 | tf_op jit(solution)/shard_map/all_gather | solution.py:21
  514.0 0.8 copy-start.1
  516.7 76.7 %all-gather.33.cloned.1.call-start = ((), (), s32[]{:S(2)}) async-start(), calls=%async_computation.10 | async-start | bytes 2162688 | tf_op jit(solution)/shard_map/all_gather | solution.py:28
  518.4 112.9 %all-gather.35.cloned.1.call-start = ((), (), s32[]{:S(2)}) async-start(), calls=%async_computation.11 | async-start | bytes 2621440 | tf_op jit(solution)/shard_map/all_gather | solution.py:21
  598.3 0.8 copy-start.5
  601.3 76.7 %all-gather.37.cloned.1.call-start = ((), (), s32[]{:S(2)}) async-start(), calls=%async_computation.12 | async-start | bytes 2162688 | tf_op jit(solution)/shard_map/all_gather | solution.py:28
  603.0 223.0 %all-reduce.6.cloned.1.call-start = ((), (), s32[]{:S(2)}) async-start(), calls=%async_computation.13 | async-start | bytes 131072 | tf_op jit(solution)/shard_map/psum | solution.py:85
  684.6 0.8 copy-start.3
  687.0 194.1 %all-gather.39.cloned.1.call-start = ((), (), s32[]{:S(2)}) async-start(), calls=%async_computation.14 | async-start | bytes 2621440 | tf_op jit(solution)/shard_map/all_gather | solution.py:21
  853.3 74.4 %all-gather.41.cloned.1.call-start = ((), (), s32[]{:S(2)}) async-start(), calls=%async_computation.15 | async-start | bytes 2162688 | tf_op jit(solution)/shard_map/all_gather | solution.py:28
  855.0 219.5 %all-reduce.8.cloned.1.call-start = ((), (), s32[]{:S(2)}) async-start(), calls=%async_computation.16 | async-start | bytes 131072 | tf_op jit(solution)/shard_map/psum | solution.py:89
Sparse Core Ops, SparseCore 0:
  9.6 34.0 all-gather.14
  46.5 43.8 all-gather.16
  98.3 29.7 all-gather.18
  130.8 43.8 all-gather.20
  182.7 29.7 all-gather.22
  215.2 43.8 all-gather.24
  268.3 138.7 all-reduce.3
  434.6 27.6 all-gather.26
  465.1 43.8 all-gather.28
  516.9 29.7 all-gather.30
  549.5 43.8 all-gather.32
  601.5 29.7 all-gather.34
  634.1 43.8 all-gather.36
  687.1 138.7 all-reduce.5
  853.4 27.6 all-gather.38
  883.9 43.8 all-gather.40
  935.7 138.7 all-reduce.7
where the time goes:
time: 1090 us; the launch traced here: 1080 us
  waiting for transfers between devices  819 us (75%)
  other arithmetic  95.5 us (9%)
  matrix products  82.2 us (8%)
  local copies, waits for them, and re-layouts  68.7 us (6%)
  between operations  15.2 us (1%)
    psum x2, waiting for transfers between devices, local(): gram = lax.psum(inner(filtered, filtered), ('dom', 'near')) / nodes_all  277 us
    all_gather x7, waiting for transfers between devices, apply_operator(): lax.all_gather(edge_tile, 'dom', axis=0, tiled=True)  207 us
    all_gather x7, waiting for transfers between devices, apply_operator(): gathered = lax.all_gather(block, 'near', axis=0, tiled=True)  196 us
    psum x1, waiting for transfers between devices, local(): lax.psum(inner(current, final_image), ('dom', 'near')) / nodes_all  139 us
    dot_general x7, matrix products, apply_operator(): jnp.einsum('sij,sjk->sik', near_tiles, picked, precision=lax.Precision.HI...  56.9 us
    gather x7, local copies, waits for them, and re-layouts, apply_operator(): gathered.reshape(group_size * tiles_dev, tile_rows, width)[near_src]  28 us
    another operation x6, other arithmetic, inverse_factor(): lower = jnp.linalg.cholesky(gram)  24.8 us
  transfers between devices with their start and end apart: 17, of which 17 were waited for; matrix products, arithmetic and copies ran while one was open for 12% of the time, Pallas kernels for 0%

commit v1 on v0

--- a/solution.py
+++ b/solution.py
@@ -11,6 +11,16 @@
 UPPER_EDGE = 2.0
 
 
+def turned_line(array, axis, dim):
+    peers = lax.axis_size(axis)
+    current, parts = (array, [array])
+    for _ in range(peers - 1):
+        current = lax.ppermute(current, axis, [(i, (i + 1) % peers) for i in range(peers)])
+        parts.insert(0, current)
+    flat = jnp.concatenate(parts, axis=dim)
+    return jnp.roll(flat, (lax.axis_index(axis) + 1) * array.shape[dim], axis=dim)
+
+
 def apply_operator(
     block, near_tiles, near_src, near_mask, far_tiles, far_src, far_mask, bound_count
 ):
@@ -18,7 +28,7 @@
     width = block.shape[1]
     tiles_dev = block.shape[0] // tile_rows
     group_size = lax.axis_size("near")
-    gathered = lax.all_gather(block, "near", axis=0, tiled=True)
+    gathered = turned_line(block, "near", 0)
     picked = gathered.reshape(group_size * tiles_dev, tile_rows, width)[near_src]
     products = jnp.einsum("sij,sjk->sik", near_tiles, picked, precision=lax.Precision.HIGHEST)
     products = products * near_mask.astype(jnp.float32)[:, None, None]

time: 1090 us -> 1000 us (0.917)
  waiting for transfers between devices: 819 us -> 680 us
  other arithmetic: 95.5 us -> 132 us
    ppermute x0 -> x21, waiting for transfers between devices: none -> 254 us  [turned_line(): lax.ppermute(current, axis, [(i, (i + 1) % peers) for i in range(peers)])]
    all_gather x7, waiting for transfers between devices: 207 us -> 0.01 us  [apply_operator(): lax.all_gather(edge_tile, 'dom', axis=0, tiled=True)]
    all_gather x7 -> x0, waiting for transfers between devices: 196 us -> none  [apply_operator(): gathered = lax.all_gather(block, 'near', axis=0, tiled=True)]
    concatenate x0 -> x7, other arithmetic: none -> 45.2 us  [turned_line(): jnp.roll(flat, (lax.axis_index(axis) + 1) * array.shape[dim], axis=dim)]
    psum x2, waiting for transfers between devices: 277 us -> 289 us  [local(): gram = lax.psum(inner(filtered, filtered), ('dom', 'near')) / nodes_all]
  transfers between devices with their start and end apart: 17 -> 31, of which waited for: 17 -> 24; matrix products, arithmetic and copies ran while one was open for 12% -> 17% of each run, Pallas kernels for 0% -> 0%
where the time goes in v1:
time: 1000 us; the launch traced here: 994 us
  waiting for transfers between devices  680 us (68%)
  other arithmetic  132 us (13%)
  matrix products  80.6 us (8%)
  local copies, waits for them, and re-layouts  74.2 us (7%)
  between operations  15.8 us (2%)
  starting transfers between devices  10.8 us (1%)
    psum x2, waiting for transfers between devices, local(): gram = lax.psum(inner(filtered, filtered), ('dom', 'near')) / nodes_all  289 us
    ppermute x21, waiting for transfers between devices, turned_line(): lax.ppermute(current, axis, [(i, (i + 1) % peers) for i in range(peers)])  254 us
    psum x1, waiting for transfers between devices, local(): lax.psum(inner(current, final_image), ('dom', 'near')) / nodes_all  137 us
    dot_general x7, matrix products, apply_operator(): jnp.einsum('sij,sjk->sik', near_tiles, picked, precision=lax.Precision.HI...  56.8 us
    concatenate x7, other arithmetic, turned_line(): jnp.roll(flat, (lax.axis_index(axis) + 1) * array.shape[dim], axis=dim)  45.2 us
    gather x7, local copies, waits for them, and re-layouts, apply_operator(): gathered.reshape(group_size * tiles_dev, tile_rows, width)[near_src]  27.9 us
    another operation x6, other arithmetic, inverse_factor(): lower = jnp.linalg.cholesky(gram)  24.8 us
    another operation x4, other arithmetic, inverse_factor(): jax.scipy.linalg.solve_triangular(lower, jnp.eye(gram.shape[0], dtype=jnp...  20.9 us
  transfers between devices with their start and end apart: 31, of which 24 were waited for; matrix products, arithmetic and copies ran while one was open for 17% of the time, Pallas kernels for 0%

profile of v1, /device:TPU:1, one launch (start us, length us, event | category | flops | bytes accessed | tf_op | source)
XLA Modules:
  0.0 994.0 jit_solution(772266820513304977)
XLA Ops:
  12.3 14.0 %collective-permute-done = f32[1024,128]{1,0:T(8,128)S(1)} collective-permute-done((f32[1024,128]{1,0:T(8,128)}, f32[1024,128]{1,0:T(8,128)S(1)}, u32[]{:S(2)}, u32[]{:S(2)}) %collective-permute-start) | collective-permute-done | bytes 524320 | tf_op jit(solution)/shard_map/ppermute | solution.py:18
  27.0 13.5 %collective-permute-done.1 = f32[1024,128]{1,0:T(8,128)} collective-permute-done((f32[1024,128]{1,0:T(8,128)S(1)}, f32[1024,128]{1,0:T(8,128)}, u32[]{:S(2)}, u32[]{:S(2)}) %collective-permute-start.1) | collective-permute-done | bytes 524320 | tf_op jit(solution)/shard_map/ppermute | solution.py:18
  43.2 10.3 %collective-permute-done.2 = f32[1024,128]{1,0:T(8,128)} collective-permute-done((f32[1024,128]{1,0:T(8,128)}, f32[1024,128]{1,0:T(8,128)}, u32[]{:S(2)}, u32[]{:S(2)}) %collective-permute-start.2) | collective-permute-done | bytes 524320 | tf_op jit(solution)/shard_map/ppermute | solution.py:18
  84.5 11.9 %collective-permute-done.3 = f32[1024,128]{1,0:T(8,128)S(1)} collective-permute-done((f32[1024,128]{1,0:T(8,128)}, f32[1024,128]{1,0:T(8,128)S(1)}, u32[]{:S(2)}, u32[]{:S(2)}) %collective-permute-start.3) | collective-permute-done | bytes 524320 | tf_op jit(solution)/shard_map/ppermute | solution.py:18
  96.4 10.8 %collective-permute-done.4 = f32[1024,128]{1,0:T(8,128)S(1)} collective-permute-done((f32[1024,128]{1,0:T(8,128)S(1)}, f32[1024,128]{1,0:T(8,128)S(1)}, u32[]{:S(2)}, u32[]{:S(2)}) %collective-permute-start.4) | collective-permute-done | bytes 524320 | tf_op jit(solution)/shard_map/ppermute | solution.py:18
  159.5 12.0 %collective-permute-done.7 = f32[1024,128]{1,0:T(8,128)S(1)} collective-permute-done((f32[1024,128]{1,0:T(8,128)S(1)}, f32[1024,128]{1,0:T(8,128)S(1)}, u32[]{:S(2)}, u32[]{:S(2)}) %collective-permute-start.7) | collective-permute-done | bytes 524320 | tf_op jit(solution)/shard_map/ppermute | solution.py:18
  171.8 12.1 %collective-permute-done.8 = f32[1024,128]{1,0:T(8,128)S(1)} collective-permute-done((f32[1024,128]{1,0:T(8,128)S(1)}, f32[1024,128]{1,0:T(8,128)S(1)}, u32[]{:S(2)}, u32[]{:S(2)}) %collective-permute-start.8) | collective-permute-done | bytes 524320 | tf_op jit(solution)/shard_map/ppermute | solution.py:18
  216.9 146.8 %all-reduce.4.cloned.1.call-done = f32[128,128]{0,1:T(8,128)} async-done(((f32[128,128]{0,1:T(8,128)}), f32[128,128]{0,1:T(8,128)}) %all-reduce.4.cloned.1.call-update) | async-done | bytes 65552 | tf_op jit(solution)/shard_map/psum | solution.py:95
  365.5 11.7 %cholesky.44 = f32[128,128]{1,0:T(8,128)S(1)} custom-call(f32[128,128]{1,0:T(8,128)S(1)} %fusion.90), custom_call_target="Cholesky" | custom-call | tf_op jit(solution)/shard_map/jit(cholesky)/cholesky | solution.py:71
  393.1 12.5 %collective-permute-done.9 = f32[1024,128]{1,0:T(8,128)S(1)} collective-permute-done((f32[1024,128]{1,0:T(8,128)}, f32[1024,128]{1,0:T(8,128)S(1)}, u32[]{:S(2)}, u32[]{:S(2)}) %collective-permute-start.9) | collective-permute-done | bytes 524320 | tf_op jit(solution)/shard_map/ppermute | solution.py:18
  407.2 13.5 %collective-permute-done.10 = f32[1024,128]{1,0:T(8,128)S(1)} collective-permute-done((f32[1024,128]{1,0:T(8,128)S(1)}, f32[1024,128]{1,0:T(8,128)S(1)}, u32[]{:S(2)}, u32[]{:S(2)}) %collective-permute-start.10) | collective-permute-done | bytes 524320 | tf_op jit(solution)/shard_map/ppermute | solution.py:18
  420.9 14.2 %collective-permute-done.11 = f32[1024,128]{1,0:T(8,128)S(1)} collective-permute-done((f32[1024,128]{1,0:T(8,128)S(1)}, f32[1024,128]{1,0:T(8,128)S(1)}, u32[]{:S(2)}, u32[]{:S(2)}) %collective-permute-start.11) | collective-permute-done | bytes 524320 | tf_op jit(solution)/shard_map/ppermute | solution.py:18
  467.3 13.5 %collective-permute-done.12 = f32[1024,128]{1,0:T(8,128)S(1)} collective-permute-done((f32[1024,128]{1,0:T(8,128)}, f32[1024,128]{1,0:T(8,128)S(1)}, u32[]{:S(2)}, u32[]{:S(2)}) %collective-permute-start.12) | collective-permute-done | bytes 524320 | tf_op jit(solution)/shard_map/ppermute | solution.py:18
  480.9 12.5 %collective-permute-done.13 = f32[1024,128]{1,0:T(8,128)S(1)} collective-permute-done((f32[1024,128]{1,0:T(8,128)S(1)}, f32[1024,128]{1,0:T(8,128)S(1)}, u32[]{:S(2)}, u32[]{:S(2)}) %collective-permute-start.13) | collective-permute-done | bytes 524320 | tf_op jit(solution)/shard_map/ppermute | solution.py:18
  493.7 11.6 %collective-permute-done.14 = f32[1024,128]{1,0:T(8,128)S(1)} collective-permute-done((f32[1024,128]{1,0:T(8,128)S(1)}, f32[1024,128]{1,0:T(8,128)S(1)}, u32[]{:S(2)}, u32[]{:S(2)}) %collective-permute-start.14) | collective-permute-done | bytes 524320 | tf_op jit(solution)/shard_map/ppermute | solution.py:18
  537.8 11.0 %collective-permute-done.15 = f32[1024,128]{1,0:T(8,128)S(1)} collective-permute-done((f32[1024,128]{1,0:T(8,128)}, f32[1024,128]{1,0:T(8,128)S(1)}, u32[]{:S(2)}, u32[]{:S(2)}) %collective-permute-start.15) | collective-permute-done | bytes 524320 | tf_op jit(solution)/shard_map/ppermute | solution.py:18
  548.8 10.5 %collective-permute-done.16 = f32[1024,128]{1,0:T(8,128)S(1)} collective-permute-done((f32[1024,128]{1,0:T(8,128)S(1)}, f32[1024,128]{1,0:T(8,128)S(1)}, u32[]{:S(2)}, u32[]{:S(2)}) %collective-permute-start.16) | collective-permute-done | bytes 524320 | tf_op jit(solution)/shard_map/ppermute | solution.py:18
  559.4 10.3 %collective-permute-done.17 = f32[1024,128]{1,0:T(8,128)S(1)} collective-permute-done((f32[1024,128]{1,0:T(8,128)S(1)}, f32[1024,128]{1,0:T(8,128)S(1)}, u32[]{:S(2)}, u32[]{:S(2)}) %collective-permute-start.17) | collective-permute-done | bytes 524320 | tf_op jit(solution)/shard_map/ppermute | solution.py:18
  602.7 141.8 %all-reduce.6.cloned.1.call-done = f32[128,128]{0,1:T(8,128)} async-done(((f32[128,128]{0,1:T(8,128)}), f32[128,128]{0,1:T(8,128)}) %all-reduce.6.cloned.1.call-update) | async-done | bytes 65552 | tf_op jit(solution)/shard_map/psum | solution.py:95
  746.4 11.7 %cholesky.55 = f32[128,128]{1,0:T(8,128)S(1)} custom-call(f32[128,128]{1,0:T(8,128)S(1)} %fusion.88), custom_call_target="Cholesky" | custom-call | tf_op jit(solution)/shard_map/jit(cholesky)/cholesky | solution.py:71
  774.0 12.5 %collective-permute-done.18 = f32[1024,128]{1,0:T(8,128)S(1)} collective-permute-done((f32[1024,128]{1,0:T(8,128)}, f32[1024,128]{1,0:T(8,128)S(1)}, u32[]{:S(2)}, u32[]{:S(2)}) %collective-permute-start.18) | collective-permute-done | bytes 524320 | tf_op jit(solution)/shard_map/ppermute | solution.py:18
  788.1 13.5 %collective-permute-done.19 = f32[1024,128]{1,0:T(8,128)S(1)} collective-permute-done((f32[1024,128]{1,0:T(8,128)S(1)}, f32[1024,128]{1,0:T(8,128)S(1)}, u32[]{:S(2)}, u32[]{:S(2)}) %collective-permute-start.19) | collective-permute-done | bytes 524320 | tf_op jit(solution)/shard_map/ppermute | solution.py:18
  801.8 14.2 %collective-permute-done.20 = f32[1024,128]{1,0:T(8,128)S(1)} collective-permute-done((f32[1024,128]{1,0:T(8,128)S(1)}, f32[1024,128]{1,0:T(8,128)S(1)}, u32[]{:S(2)}, u32[]{:S(2)}) %collective-permute-start.20) | collective-permute-done | bytes 524320 | tf_op jit(solution)/shard_map/ppermute | solution.py:18
  847.7 137.5 %all-reduce.8.cloned.1.call-done = f32[128,128]{0,1:T(8,128)} async-done(((f32[128,128]{0,1:T(8,128)}), f32[128,128]{0,1:T(8,128)}) %all-reduce.8.cloned.1.call-update) | async-done | bytes 65552 | tf_op jit(solution)/shard_map/psum | solution.py:99
  (170 shorter events, 294.4 us)
Async XLA Ops:
  7.2 68.7 %all-gather.8.cloned.1.call-start = ((), (), s32[]{:S(2)}) async-start(), calls=%async_computation | async-start | bytes 2162688 | tf_op jit(solution)/shard_map/all_gather | solution.py:38
  9.7 131.6 %all-gather.10.cloned.1.call-start = ((), (), s32[]{:S(2)}) async-start(), calls=%async_computation.1 | async-start | bytes 2162688 | tf_op jit(solution)/shard_map/all_gather | solution.py:38
  9.8 16.5 %collective-permute-start = (f32[1024,128]{1,0:T(8,128)}, f32[1024,128]{1,0:T(8,128)S(1)}, u32[]{:S(2)}, u32[]{:S(2)}) collective-permute-start(f32[1024,128]{1,0:T(8,128)} %param.13), channel_id=1, source_target_pairs={{0,1},{1,2},{2,3},{3,0},{4,5},{5,6},{6,7},{7,4},{8,9},{9,10},{10,1... | collective-permute-start | bytes 1572872 | tf_op jit(solution)/shard_map/ppermute | solution.py:18
  27.0 13.5 %collective-permute-start.1 = (f32[1024,128]{1,0:T(8,128)S(1)}, f32[1024,128]{1,0:T(8,128)}, u32[]{:S(2)}, u32[]{:S(2)}) collective-permute-start(f32[1024,128]{1,0:T(8,128)S(1)} %collective-permute-done), channel_id=1, source_target_pairs={{0,1},{1,2},{2,3},{3,0},{4,5},{5,6},{6,7},{7,4},{8,9},{9,10},{10,1... | collective-permute-start | bytes 1572872 | tf_op jit(solution)/shard_map/ppermute | solution.py:18
  40.6 12.9 %collective-permute-start.2 = (f32[1024,128]{1,0:T(8,128)}, f32[1024,128]{1,0:T(8,128)}, u32[]{:S(2)}, u32[]{:S(2)}) collective-permute-start(f32[1024,128]{1,0:T(8,128)} %collective-permute-done.1), channel_id=1, source_target_pairs={{0,1},{1,2},{2,3},{3,0},{4,5},{5,6},{6,7},{7,4},{8,9},{9,10},{10,1... | collective-permute-start | bytes 1572872 | tf_op jit(solution)/shard_map/ppermute | solution.py:18
  84.3 123.3 %all-gather.12.cloned.1.call-start = ((), (), s32[]{:S(2)}) async-start(), calls=%async_computation.2 | async-start | bytes 2162688 | tf_op jit(solution)/shard_map/all_gather | solution.py:38
  84.4 12.0 %collective-permute-start.3 = (f32[1024,128]{1,0:T(8,128)}, f32[1024,128]{1,0:T(8,128)S(1)}, u32[]{:S(2)}, u32[]{:S(2)}) collective-permute-start(f32[1024,128]{1,0:T(8,128)} %copy-done.9), channel_id=1, source_target_pairs={{0,1},{1,2},{2,3},{3,0},{4,5},{5,6},{6,7},{7,4},{8,9},{9,10},{10,1... | collective-permute-start | bytes 1572872 | tf_op jit(solution)/shard_map/ppermute | solution.py:18
  149.9 213.8 %all-reduce.4.cloned.1.call-start = ((), (), s32[]{:S(2)}) async-start(), calls=%async_computation.3 | async-start | bytes 131072 | tf_op jit(solution)/shard_map/psum | solution.py:95
  171.4 12.5 %collective-permute-start.8 = (f32[1024,128]{1,0:T(8,128)S(1)}, f32[1024,128]{1,0:T(8,128)S(1)}, u32[]{:S(2)}, u32[]{:S(2)}) collective-permute-start(f32[1024,128]{1,0:T(8,128)S(1)} %collective-permute-done.7), channel_id=1, source_target_pairs={{0,1},{1,2},{2,3},{3,0},{4,5},{5,6},{6,7},{7,4},{8,9},{9,10},{10,1... | collective-permute-start | bytes 1572872 | tf_op jit(solution)/shard_map/ppermute | solution.py:18
  216.6 242.1 %all-gather.14.cloned.1.call-start = ((), (), s32[]{:S(2)}) async-start(), calls=%async_computation.4 | async-start | bytes 2162688 | tf_op jit(solution)/shard_map/all_gather | solution.py:38
  391.8 137.2 %all-gather.16.cloned.1.call-start = ((), (), s32[]{:S(2)}) async-start(), calls=%async_computation.5 | async-start | bytes 2162688 | tf_op jit(solution)/shard_map/all_gather | solution.py:38
  391.9 13.7 %collective-permute-start.9 = (f32[1024,128]{1,0:T(8,128)}, f32[1024,128]{1,0:T(8,128)S(1)}, u32[]{:S(2)}, u32[]{:S(2)}) collective-permute-start(f32[1024,128]{1,0:T(8,128)} %copy-done.1), channel_id=1, source_target_pairs={{0,1},{1,2},{2,3},{3,0},{4,5},{5,6},{6,7},{7,4},{8,9},{9,10},{10,1... | collective-permute-start | bytes 1572872 | tf_op jit(solution)/shard_map/ppermute | solution.py:18
  405.6 15.1 %collective-permute-start.10 = (f32[1024,128]{1,0:T(8,128)S(1)}, f32[1024,128]{1,0:T(8,128)S(1)}, u32[]{:S(2)}, u32[]{:S(2)}) collective-permute-start(f32[1024,128]{1,0:T(8,128)S(1)} %collective-permute-done.9), channel_id=1, source_target_pairs={{0,1},{1,2},{2,3},{3,0},{4,5},{5,6},{6,7},{7,4},{8,9},{9,10},{10,1... | collective-permute-start | bytes 1572872 | tf_op jit(solution)/shard_map/ppermute | solution.py:18
  420.7 14.4 %collective-permute-start.11 = (f32[1024,128]{1,0:T(8,128)S(1)}, f32[1024,128]{1,0:T(8,128)S(1)}, u32[]{:S(2)}, u32[]{:S(2)}) collective-permute-start(f32[1024,128]{1,0:T(8,128)S(1)} %collective-permute-done.10), channel_id=1, source_target_pairs={{0,1},{1,2},{2,3},{3,0},{4,5},{5,6},{6,7},{7,4},{8,9},{9,10},{10,1... | collective-permute-start | bytes 1572872 | tf_op jit(solution)/shard_map/ppermute | solution.py:18
  467.2 126.3 %all-gather.18.cloned.1.call-start = ((), (), s32[]{:S(2)}) async-start(), calls=%async_computation.6 | async-start | bytes 2162688 | tf_op jit(solution)/shard_map/all_gather | solution.py:38
  467.2 13.6 %collective-permute-start.12 = (f32[1024,128]{1,0:T(8,128)}, f32[1024,128]{1,0:T(8,128)S(1)}, u32[]{:S(2)}, u32[]{:S(2)}) collective-permute-start(f32[1024,128]{1,0:T(8,128)} %copy-done.10), channel_id=1, source_target_pairs={{0,1},{1,2},{2,3},{3,0},{4,5},{5,6},{6,7},{7,4},{8,9},{9,10},{10,1... | collective-permute-start | bytes 1572872 | tf_op jit(solution)/shard_map/ppermute | solution.py:18
  480.9 12.5 %collective-permute-start.13 = (f32[1024,128]{1,0:T(8,128)S(1)}, f32[1024,128]{1,0:T(8,128)S(1)}, u32[]{:S(2)}, u32[]{:S(2)}) collective-permute-start(f32[1024,128]{1,0:T(8,128)S(1)} %collective-permute-done.12), channel_id=1, source_target_pairs={{0,1},{1,2},{2,3},{3,0},{4,5},{5,6},{6,7},{7,4},{8,9},{9,10},{10,1... | collective-permute-start | bytes 1572872 | tf_op jit(solution)/shard_map/ppermute | solution.py:18
  493.3 12.0 %collective-permute-start.14 = (f32[1024,128]{1,0:T(8,128)S(1)}, f32[1024,128]{1,0:T(8,128)S(1)}, u32[]{:S(2)}, u32[]{:S(2)}) collective-permute-start(f32[1024,128]{1,0:T(8,128)S(1)} %collective-permute-done.13), channel_id=1, source_target_pairs={{0,1},{1,2},{2,3},{3,0},{4,5},{5,6},{6,7},{7,4},{8,9},{9,10},{10,1... | collective-permute-start | bytes 1572872 | tf_op jit(solution)/shard_map/ppermute | solution.py:18
  537.7 206.9 %all-reduce.6.cloned.1.call-start = ((), (), s32[]{:S(2)}) async-start(), calls=%async_computation.7 | async-start | bytes 131072 | tf_op jit(solution)/shard_map/psum | solution.py:95
  602.5 237.2 %all-gather.20.cloned.1.call-start = ((), (), s32[]{:S(2)}) async-start(), calls=%async_computation.8 | async-start | bytes 2162688 | tf_op jit(solution)/shard_map/all_gather | solution.py:38
  772.7 212.4 %all-reduce.8.cloned.1.call-start = ((), (), s32[]{:S(2)}) async-start(), calls=%async_computation.9 | async-start | bytes 131072 | tf_op jit(solution)/shard_map/psum | solution.py:99
  772.8 13.7 %collective-permute-start.18 = (f32[1024,128]{1,0:T(8,128)}, f32[1024,128]{1,0:T(8,128)S(1)}, u32[]{:S(2)}, u32[]{:S(2)}) collective-permute-start(f32[1024,128]{1,0:T(8,128)} %copy-done.2), channel_id=1, source_target_pairs={{0,1},{1,2},{2,3},{3,0},{4,5},{5,6},{6,7},{7,4},{8,9},{9,10},{10,1... | collective-permute-start | bytes 1572872 | tf_op jit(solution)/shard_map/ppermute | solution.py:18
  786.5 15.1 %collective-permute-start.19 = (f32[1024,128]{1,0:T(8,128)S(1)}, f32[1024,128]{1,0:T(8,128)S(1)}, u32[]{:S(2)}, u32[]{:S(2)}) collective-permute-start(f32[1024,128]{1,0:T(8,128)S(1)} %collective-permute-done.18), channel_id=1, source_target_pairs={{0,1},{1,2},{2,3},{3,0},{4,5},{5,6},{6,7},{7,4},{8,9},{9,10},{10,1... | collective-permute-start | bytes 1572872 | tf_op jit(solution)/shard_map/ppermute | solution.py:18
  801.5 14.4 %collective-permute-start.20 = (f32[1024,128]{1,0:T(8,128)S(1)}, f32[1024,128]{1,0:T(8,128)S(1)}, u32[]{:S(2)}, u32[]{:S(2)}) collective-permute-start(f32[1024,128]{1,0:T(8,128)S(1)} %collective-permute-done.19), channel_id=1, source_target_pairs={{0,1},{1,2},{2,3},{3,0},{4,5},{5,6},{6,7},{7,4},{8,9},{9,10},{10,1... | collective-permute-start | bytes 1572872 | tf_op jit(solution)/shard_map/ppermute | solution.py:18
  (21 other events, 140.8 us)
Sparse Core Ops, SparseCore 0:
  10.8 47.0 all-gather.7
  84.4 45.0 all-gather.9
  150.0 47.8 all-gather.11
  216.8 146.8 all-reduce.3
  391.9 40.6 all-gather.13
  467.3 41.3 all-gather.15
  537.8 43.1 all-gather.17
  602.6 141.9 all-reduce.5
  772.8 40.6 all-gather.19
  847.8 137.3 all-reduce.7
